TPU v7x, 128 devices: a whole 4x4x4 slice. The times are simulated.
128 devices in a mesh: lat: 16 (over x, z), dep: 8 (over y, core).
Axes of the slice: x: 4, y: 4, z: 4, core: 2. Of those that a mesh axis runs over, the one named last changes fastest.
Arguments:
- state: float32 [64, 64, 128], P('lat', 'dep'), may hold values from 0.2 to 1
- kappa: float32 [64, 64, 128], P('lat', 'dep'), may hold values from 0.3 to 3
- rate: float32 [64, 64], P('lat', 'dep'), may hold values from 1 to 4
- grads: float32 [3, 64, 64], replicated, may hold values from -0.75 to 0.75
- lift: float32 [4, 32, 128], replicated, may hold values from -0.375 to 0.375
- rhs: float32 [64, 64, 32, 128], P('lat', 'dep'), may hold values from -18 to 18
Outputs:
- update: float32 [64, 64, 32, 128], P('lat', 'dep')
All inputs are finite; a program needn't handle non-finite values.
Results may differ from a plain program's by a relative error of at most 0.0003.
Values sent between devices are 32-bit elements; how exact they have to be, the bound alone decides.
A program may use at most 128 MiB of HBM per device.

v0:
```python
import jax
import jax.numpy as jnp
from jax import lax
from jax.sharding import PartitionSpec as P

KRY = 8
highest = lax.Precision.HIGHEST
mass_shift = 0.25


def with_halo(cells, sides, width, closed):
    for axis, dim in sides:
        count = lax.axis_size(axis)
        ends = count if closed else count - 1
        head = lax.slice_in_dim(cells, 0, width, axis=dim)
        tail = lax.slice_in_dim(cells, cells.shape[dim] - width, cells.shape[dim], axis=dim)
        cells = jnp.concatenate(
            [
                lax.ppermute(tail, axis, [(i, (i + 1) % count) for i in range(ends)]),
                cells,
                lax.ppermute(head, axis, [((i + 1) % count, i) for i in range(ends)]),
            ],
            axis=dim,
        )
    return cells


def from_behind(value, axis, steps):
    count = lax.axis_size(axis)
    pairs = [(source, (source + steps) % count) for source in range(count)]
    return lax.ppermute(value, axis, pairs)


def passed_along(array, axis, by):
    peers = lax.axis_size(axis)
    pairs = [(i, i + by) for i in range(peers) if 0 <= i + by < peers]
    return lax.ppermute(array, axis, pairs)


def face_table():
    unknown = jnp.arange(128, dtype=jnp.int32)[:, None]
    column = jnp.arange(128, dtype=jnp.int32)[None, :]
    face_id = column // 32
    species = column // 16 % 2
    along_one = column % 16 // 4
    along_two = column % 4
    edge_pos = 3 * (face_id % 2)
    is_lateral = face_id < 2
    node_x = jnp.where(is_lateral, edge_pos, along_one)
    node_y = jnp.where(is_lateral, along_one, along_two)
    node_z = jnp.where(is_lateral, along_two, edge_pos)
    target = species * 64 + node_x * 16 + node_y * 4 + node_z
    return (unknown == target).astype(jnp.float32)


def pairing_table():
    unknown = jnp.arange(128, dtype=jnp.int32)
    return (unknown[:, None] % 64 == unknown[None, :] % 64).astype(jnp.float32)


def element_tiles(kappa_rows, state_rows, rate_rows, grads, select):
    row_count = kappa_rows.shape[0]
    split_kappa = kappa_rows.reshape(row_count, 2, 64)
    stiffness = jnp.einsum("dqi,nsq,dqj->nsij", grads, split_kappa, grads, precision=highest)
    zero_block = jnp.zeros((row_count, 64, 64), jnp.float32)
    top_half = jnp.concatenate([stiffness[:, 0], zero_block], axis=2)
    bottom_half = jnp.concatenate([zero_block, stiffness[:, 1]], axis=2)
    face_kappa = jnp.dot(kappa_rows, select, precision=highest)
    penalty = jnp.dot(face_kappa, select.T, precision=highest)
    partner = jnp.concatenate([state_rows[:, 64:], state_rows[:, :64]], axis=1)
    identity = jnp.eye(128, dtype=jnp.float32)
    diag_tiles = jnp.concatenate([top_half, bottom_half], axis=1)
    diag_tiles = diag_tiles + identity[None] * (mass_shift + penalty)[:, None, :]
    diag_tiles = diag_tiles + pairing_table()[None] * (rate_rows[:, None] * partner)[:, None, :]
    return (diag_tiles, face_kappa)


def apply_operator(vectors, diag_tiles, couple, select):
    lat_rows = vectors.shape[0]
    dep_rows = vectors.shape[1]
    columns = vectors.shape[2]
    traces = jnp.einsum("aevu,uk->aevk", vectors, select, precision=highest)
    lat_rims = jnp.stack([traces[0, :, :, 0:32], traces[-1, :, :, 32:64]]).reshape(
        2, dep_rows, columns * 32
    )
    lat_wide = with_halo(lat_rims, (("lat", 0),), 1, True)
    prev_lat = lat_wide[0].reshape(dep_rows, columns, 32)
    next_lat = lat_wide[3].reshape(dep_rows, columns, 32)
    dep_rims = jnp.stack([traces[:, 0, :, 64:96], traces[:, -1, :, 96:128]]).reshape(
        2, lat_rows, columns * 32
    )
    dep_wide = with_halo(dep_rims, (("dep", 0),), 1, False)
    prev_dep = dep_wide[0].reshape(lat_rows, columns, 32)
    next_dep = dep_wide[3].reshape(lat_rows, columns, 32)
    from_left = jnp.concatenate([prev_lat[None], traces[:-1, :, :, 32:64]], axis=0)
    from_right = jnp.concatenate([traces[1:, :, :, 0:32], next_lat[None]], axis=0)
    from_below = jnp.concatenate([prev_dep[:, None], traces[:, :-1, :, 96:128]], axis=1)
    from_above = jnp.concatenate([traces[:, 1:, :, 64:96], next_dep[:, None]], axis=1)
    near_traces = jnp.concatenate([from_left, from_right, from_below, from_above], axis=-1)
    own_part = jnp.einsum("aeij,aevj->aevi", diag_tiles, vectors, precision=highest)
    coupled = jnp.einsum("aeki,aevk->aevi", couple, near_traces, precision=highest)
    return own_part - coupled


def inner_local(left_block, right_block):
    return jnp.einsum("aevu,aewu->vw", left_block, right_block, precision=highest)


def combine_columns(vectors, matrix):
    return jnp.einsum("aevu,vw->aewu", vectors, matrix, precision=highest)


def factor(gram_matrix):
    lower_factor = jnp.linalg.cholesky(gram_matrix)
    identity = jnp.eye(gram_matrix.shape[0], dtype=gram_matrix.dtype)
    inverse = jax.scipy.linalg.solve_triangular(lower_factor, identity, lower=True)
    return (lower_factor.T, inverse.T)


def per_device(state, kappa, rate, grads, lift, rhs):
    select = face_table()

    def one_row(row_data):
        return element_tiles(row_data[0], row_data[1], row_data[2], grads, select)

    diag_tiles, face_kappa = lax.map(one_row, (kappa, state, rate))
    lat_end = face_kappa[-1, :, 32:64]
    dep_end = face_kappa[:, -1, 96:128]
    own_right = lift[1] * face_kappa[:, :, 32:64, None]
    own_top = lift[3] * face_kappa[:, :, 96:128, None]
    sent_lat = from_behind(lift[0][None] * lat_end[:, :, None], "lat", 1)
    sent_dep = passed_along(lift[2][None] * dep_end[:, :, None], "dep", 1)
    left_tiles = jnp.concatenate(
        [sent_lat[None], lift[0] * face_kappa[:-1, :, 32:64, None]], axis=0
    )
    below_tiles = jnp.concatenate(
        [sent_dep[:, None], lift[2] * face_kappa[:, :-1, 96:128, None]], axis=1
    )
    couple = jnp.concatenate([left_tiles, own_right, below_tiles, own_top], axis=2)
    columns = rhs.shape[2]
    start_factor, inverse = factor(lax.psum(inner_local(rhs, rhs), ("lat", "dep")))
    basis_list = [combine_columns(rhs, inverse)]
    coef_table = []
    for step_index in range(KRY):
        image_block = apply_operator(basis_list[step_index], diag_tiles, couple, select)
        local_prods = jnp.stack(
            [inner_local(basis_list[prior], image_block) for prior in range(step_index + 1)]
        )
        coef_stack = lax.psum(local_prods, ("lat", "dep"))
        for prior in range(step_index + 1):
            image_block = image_block - combine_columns(basis_list[prior], coef_stack[prior])
        gram_matrix = lax.psum(inner_local(image_block, image_block), ("lat", "dep"))
        upper_factor, inverse = factor(gram_matrix)
        column_coefs = [coef_stack[prior] for prior in range(step_index + 1)]
        column_coefs.append(upper_factor)
        coef_table.append(column_coefs)
        basis_list.append(combine_columns(image_block, inverse))
    zero_small = jnp.zeros((columns, columns), jnp.float32)
    block_rows = []
    for row_index in range(KRY + 1):
        row_blocks = []
        for col_index in range(KRY):
            if row_index <= col_index + 1:
                row_blocks.append(coef_table[col_index][row_index])
            else:
                row_blocks.append(zero_small)
        block_rows.append(jnp.concatenate(row_blocks, axis=1))
    hessenberg = jnp.concatenate(block_rows, axis=0)
    gram_small = jnp.dot(hessenberg.T, hessenberg, precision=highest)
    right_side = jnp.dot(hessenberg[:columns].T, start_factor, precision=highest)
    coeffs = jax.scipy.linalg.cho_solve((jnp.linalg.cholesky(gram_small), True), right_side)
    update = combine_columns(basis_list[0], coeffs[:columns])
    for step_index in range(1, KRY):
        update = update + combine_columns(
            basis_list[step_index], coeffs[step_index * columns : (step_index + 1) * columns]
        )
    return update


def solution(mesh):
    in_specs = (
        P("lat", "dep", None),
        P("lat", "dep", None),
        P("lat", "dep"),
        P(),
        P(),
        P("lat", "dep", None, None),
    )
    out_specs = P("lat", "dep", None, None)
    return jax.shard_map(
        per_device, mesh=mesh, in_specs=in_specs, out_specs=out_specs, check_vma=False
    )
```

profile of v0, /device:TPU:1, one launch (start us, length us, event | category | flops | bytes accessed | tf_op | source)
XLA Modules:
  0.0 1614.5 jit_solution(5282608771596217027)
XLA Ops:
  1.6 68.8 %psum.119 = f32[32,32]{0,1:T(8,128)S(1)} all-reduce(f32[32,32]{0,1:T(8,128)S(1)} %convolution_bitcast_fusion.97), channel_id=1, replica_groups=mesh['lat'=16,'dep'=8] {'lat','dep'}, use_global_device_ids=true, to_apply=%region_0.1 | all-reduce | flops 1024 | bytes 8192 | tf_op jit(solution)/shard_map/psum | solution.py:141
  70.5 2.9 cholesky.267
  79.8 4.8 collective-permute-start.1
  85.4 3.0 collective-permute-start.2
  91.2 50.8 %while.18 = (s32[]{:T(128)}, f32[4,8,128,128]{3,2,1,0:T(8,128)S(1)}, f32[4,8,128]{2,1,0:T(8,128)S(1)}, f32[3,64,64]{2,0,1:T(4,128)S(1)}, f32[4,8,128]{2,1,0:T(8,...) while((s32[]{:T(128)}, ...), condition=%wide.region_4.7_spmd.clone.clone, body=%wide.region_3.6_spmd.clone.clone.sunk | while | flops 63704832 | bytes 7220429 | solution.py:126
  92.9 3.4 convolution_bitcast_fusion.99
  105.6 3.4 convolution_bitcast_fusion.99
  118.3 3.4 convolution_bitcast_fusion.99
  131.0 3.4 convolution_bitcast_fusion.99
  148.7 4.1 fusion.395
  156.0 3.6 collective-permute-start.5
  167.2 4.3 convolution_subtract_fusion.7
  172.6 65.2 %psum.120 = f32[32,32]{0,1:T(8,128)S(1)} all-reduce(f32[32,32]{0,1:T(8,128)} %convolution_bitcast_fusion.95), channel_id=1, replica_groups=mesh['lat'=16,'dep'=8] {'lat','dep'}, use_global_device_ids=true, to_apply=%region_5.8 | all-reduce | flops 1024 | bytes 8192 | tf_op jit(solution)/shard_map/psum | solution.py:149
  240.1 64.2 %psum.121 = f32[32,32]{0,1:T(8,128)S(1)} all-reduce(f32[32,32]{0,1:T(8,128)S(1)} %convolution_bitcast_fusion.94), channel_id=1, replica_groups=mesh['lat'=16,'dep'=8] {'lat','dep'}, use_global_device_ids=true, to_apply=%region_6.9 | all-reduce | flops 1024 | bytes 8192 | tf_op jit(solution)/shard_map/psum | solution.py:152
  304.4 2.9 cholesky.278
  315.8 4.2 fusion.396
  322.7 4.8 collective-permute-start.7
  327.5 3.5 collective-permute-start.8
  338.7 4.3 convolution_subtract_fusion.6
  344.4 62.0 %psum.122 = f32[2,32,32]{1,2,0:T(8,128)S(1)} all-reduce(f32[2,32,32]{1,2,0:T(8,128)S(1)} %pad_maximum_fusion.5), channel_id=1, replica_groups=mesh['lat'=16,'dep'=8] {'lat','dep'}, use_global_device_ids=true, to_apply=%region_7.10 | all-reduce | flops 2048 | bytes 16384 | tf_op jit(solution)/shard_map/psum | solution.py:149
  410.1 63.5 %psum.123 = f32[32,32]{0,1:T(8,128)S(1)} all-reduce(f32[32,32]{0,1:T(8,128)S(1)} %convolution_bitcast_fusion.90), channel_id=1, replica_groups=mesh['lat'=16,'dep'=8] {'lat','dep'}, use_global_device_ids=true, to_apply=%region_8.11 | all-reduce | flops 1024 | bytes 8192 | tf_op jit(solution)/shard_map/psum | solution.py:152
  473.7 2.9 cholesky.289
  485.8 4.2 fusion.397
  490.8 4.8 collective-permute-start.11
  496.6 3.2 collective-permute-start.12
  507.8 4.3 convolution_subtract_fusion.5
  513.9 62.9 %psum.124 = f32[3,32,32]{1,2,0:T(8,128)S(1)} all-reduce(f32[3,32,32]{1,2,0:T(8,128)S(1)} %pad_maximum_fusion.4), channel_id=1, replica_groups=mesh['lat'=16,'dep'=8] {'lat','dep'}, use_global_device_ids=true, to_apply=%region_9.12 | all-reduce | flops 3072 | bytes 24576 | tf_op jit(solution)/shard_map/psum | solution.py:149
  581.1 64.3 %psum.125 = f32[32,32]{0,1:T(8,128)S(1)} all-reduce(f32[32,32]{0,1:T(8,128)S(1)} %convolution_bitcast_fusion.85), channel_id=1, replica_groups=mesh['lat'=16,'dep'=8] {'lat','dep'}, use_global_device_ids=true, to_apply=%region_10.13 | all-reduce | flops 1024 | bytes 8192 | tf_op jit(solution)/shard_map/psum | solution.py:152
  645.5 2.9 cholesky.300
  657.6 4.2 fusion.398
  662.6 4.8 collective-permute-start.15
  668.4 2.9 collective-permute-start.16
  679.1 4.3 convolution_subtract_fusion.4
  685.9 63.0 %psum.126 = f32[4,32,32]{1,2,0:T(8,128)S(1)} all-reduce(f32[4,32,32]{1,2,0:T(8,128)S(1)} %pad_maximum_fusion.3), channel_id=1, replica_groups=mesh['lat'=16,'dep'=8] {'lat','dep'}, use_global_device_ids=true, to_apply=%region_11.14 | all-reduce | flops 4096 | bytes 32768 | tf_op jit(solution)/shard_map/psum | solution.py:149
  753.7 63.5 %psum.127 = f32[32,32]{0,1:T(8,128)S(1)} all-reduce(f32[32,32]{0,1:T(8,128)S(1)} %convolution_bitcast_fusion.79), channel_id=1, replica_groups=mesh['lat'=16,'dep'=8] {'lat','dep'}, use_global_device_ids=true, to_apply=%region_12.15 | all-reduce | flops 1024 | bytes 8192 | tf_op jit(solution)/shard_map/psum | solution.py:152
  817.3 2.9 cholesky.311
  830.0 4.1 fusion.399
  836.5 4.8 collective-permute-start.19
  842.2 3.5 collective-permute-start.20
  853.3 4.3 convolution_subtract_fusion.3
  860.7 62.7 %psum.128 = f32[5,32,32]{1,2,0:T(8,128)S(1)} all-reduce(f32[5,32,32]{1,2,0:T(8,128)S(1)} %fusion.76), channel_id=1, replica_groups=mesh['lat'=16,'dep'=8] {'lat','dep'}, use_global_device_ids=true, to_apply=%region_13.16 | all-reduce | flops 5120 | bytes 40960 | tf_op jit(solution)/shard_map/psum | solution.py:149
  928.8 64.2 %psum.129 = f32[32,32]{0,1:T(8,128)S(1)} all-reduce(f32[32,32]{0,1:T(8,128)S(1)} %convolution_bitcast_fusion.72), channel_id=1, replica_groups=mesh['lat'=16,'dep'=8] {'lat','dep'}, use_global_device_ids=true, to_apply=%region_14.17 | all-reduce | flops 1024 | bytes 8192 | tf_op jit(solution)/shard_map/psum | solution.py:152
  993.0 2.9 cholesky.322
  1005.8 4.1 fusion.400
  1011.7 4.8 collective-permute-start.23
  1028.7 4.3 convolution_subtract_fusion.2
  1036.6 63.3 %psum.130 = f32[6,32,32]{1,2,0:T(8,128)S(1)} all-reduce(f32[6,32,32]{1,2,0:T(8,128)S(1)} %fusion.70), channel_id=1, replica_groups=mesh['lat'=16,'dep'=8] {'lat','dep'}, use_global_device_ids=true, to_apply=%region_15.18 | all-reduce | flops 6144 | bytes 49152 | tf_op jit(solution)/shard_map/psum | solution.py:149
  1106.0 63.8 %psum.131 = f32[32,32]{0,1:T(8,128)S(1)} all-reduce(f32[32,32]{0,1:T(8,128)S(1)} %convolution_bitcast_fusion.64), channel_id=1, replica_groups=mesh['lat'=16,'dep'=8] {'lat','dep'}, use_global_device_ids=true, to_apply=%region_16.19 | all-reduce | flops 1024 | bytes 8192 | tf_op jit(solution)/shard_map/psum | solution.py:152
  1183.3 4.1 fusion.401
  1189.3 4.8 collective-permute-start.27
  1206.1 4.3 convolution_subtract_fusion.1
  1214.6 63.2 %psum.132 = f32[7,32,32]{1,2,0:T(8,128)S(1)} all-reduce(f32[7,32,32]{1,2,0:T(8,128)S(1)} %fusion.63), channel_id=1, replica_groups=mesh['lat'=16,'dep'=8] {'lat','dep'}, use_global_device_ids=true, to_apply=%region_17.20 | all-reduce | flops 7168 | bytes 57344 | tf_op jit(solution)/shard_map/psum | solution.py:149
  1284.5 64.2 %psum.133 = f32[32,32]{0,1:T(8,128)S(1)} all-reduce(f32[32,32]{0,1:T(8,128)S(1)} %convolution_bitcast_fusion.55), channel_id=1, replica_groups=mesh['lat'=16,'dep'=8] {'lat','dep'}, use_global_device_ids=true, to_apply=%region_18.21 | all-reduce | flops 1024 | bytes 8192 | tf_op jit(solution)/shard_map/psum | solution.py:152
  1361.5 4.2 fusion.402
  1367.0 4.8 collective-permute-start.31
  1381.9 4.3 convolution_subtract_fusion
  1390.9 63.0 %psum.134 = f32[8,32,32]{1,2,0:T(8,128)S(1)} all-reduce(f32[8,32,32]{1,2,0:T(8,128)S(1)} %fusion.55), channel_id=1, replica_groups=mesh['lat'=16,'dep'=8] {'lat','dep'}, use_global_device_ids=true, to_apply=%region_19.22 | all-reduce | flops 8192 | bytes 65536 | tf_op jit(solution)/shard_map/psum | solution.py:149
  1459.3 63.7 %psum.135 = f32[32,32]{0,1:T(8,128)S(1)} all-reduce(f32[32,32]{0,1:T(8,128)S(1)} %convolution_bitcast_fusion.45), channel_id=1, replica_groups=mesh['lat'=16,'dep'=8] {'lat','dep'}, use_global_device_ids=true, to_apply=%region_20.23 | all-reduce | flops 1024 | bytes 8192 | tf_op jit(solution)/shard_map/psum | solution.py:152
  1523.1 2.9 cholesky.355
  1536.6 11.7 cholesky.77
  1551.2 9.8 custom-call.23
  1563.2 11.7 cholesky.132
  1579.7 5.1 while.17
  1584.8 20.8 %custom-call.24 = f32[2,128,128]{1,2,0:T(8,128)S(1)} custom-call(f32[2,128,128]{2,1,0:T(8,128)} %get-tuple-element.122), custom_call_target="InvertDiagBlocksLowerTriangular" | custom-call | tf_op jit(solution)/shard_map/jit(_cho_solve)/triangular_solve | solution.py:171
  (645 shorter events, 310.1 us)
Async XLA Ops:
  1.0 90.0 %copy-start.76 = (f32[3,64,64]{2,1,0:T(8,128)S(1)}, f32[3,64,64]{2,1,0:T(8,128)}, u32[]{:S(2)}) copy-start(f32[3,64,64]{2,1,0:T(8,128)} %param.14) | copy-start | bytes 147460
  1.6 89.5 %copy-start.87 = (f32[4,8,128]{2,1,0:T(8,128)S(1)}, f32[4,8,128]{2,1,0:T(8,128)}, u32[]{:S(2)}) copy-start(f32[4,8,128]{2,1,0:T(8,128)} %param.12) | copy-start | bytes 49156
  73.4 3.6 copy-start.74
  78.2 12.9 copy-start.51
  79.1 84.4 %collective-permute-start = (f32[1,8,1024]{2,1,0:T(8,128)}, f32[1,8,1024]{2,1,0:T(8,128)}, u32[]{:S(2)}, u32[]{:S(2)}) collective-permute-start(f32[1,8,1024]{2,1,0:T(8,128)} %slice.619), channel_id=1, source_target_pairs={{0,8},{8,16},{16,24},{24,32},{32,40},{40,48},{48,56},{56,64},{64,7... | collective-permute-start | bytes 98312 | tf_op jit(solution)/shard_map/ppermute | solution.py:19
  79.8 85.2 %collective-permute-start.1 = (f32[1,8,1024]{2,1,0:T(8,128)}, f32[1,8,1024]{2,1,0:T(8,128)}, u32[]{:S(2)}, u32[]{:S(2)}) collective-permute-start(f32[1,8,1024]{2,1,0:T(8,128)} %slice.623), channel_id=1, source_target_pairs={{8,0},{16,8},{24,16},{32,24},{40,32},{48,40},{56,48},{64,56},{72,6... | collective-permute-start | bytes 98312 | tf_op jit(solution)/shard_map/ppermute | solution.py:21
  85.4 70.7 %collective-permute-start.2 = (f32[1,4,1024]{2,1,0:T(4,128)}, f32[1,4,1024]{2,1,0:T(4,128)S(1)}, u32[]{:S(2)}, u32[]{:S(2)}) collective-permute-start(f32[1,4,1024]{2,1,0:T(4,128)} %slice.625), channel_id=1, source_target_pairs={{0,1},{1,2},{2,3},{3,4},{4,5},{5,6},{6,7},{8,9},{9,10},{10,11},{11... | collective-permute-start | bytes 49160 | tf_op jit(solution)/shard_map/ppermute | solution.py:19
  89.1 73.0 %collective-permute-start.3 = (f32[1,4,1024]{2,1,0:T(4,128)}, f32[1,4,1024]{2,1,0:T(4,128)}, u32[]{:S(2)}, u32[]{:S(2)}) collective-permute-start(f32[1,4,1024]{2,1,0:T(4,128)} %slice.629), channel_id=1, source_target_pairs={{1,0},{2,1},{3,2},{4,3},{5,4},{6,5},{7,6},{9,8},{10,9},{11,10},{12... | collective-permute-start | bytes 49160 | tf_op jit(solution)/shard_map/ppermute | solution.py:21
  91.1 50.8 %copy-start.77 = (f32[4,32,128]{2,1,0:T(8,128)S(1)}, f32[4,32,128]{2,1,0:T(8,128)}, u32[]{:S(2)}) copy-start(f32[4,32,128]{2,1,0:T(8,128)} %param.15) | copy-start | bytes 196612
  142.0 6.7 copy-start.80
  142.0 3.6 copy-start.52
  142.8 23.7 %collective-permute-start.4 = (f32[8,32,128]{2,1,0:T(8,128)}, f32[8,32,128]{2,1,0:T(8,128)}, u32[]{:S(2)}, u32[]{:S(2)}) collective-permute-start(f32[8,32,128]{2,1,0:T(8,128)} %broadcast_multiply_fusion.4), channel_id=1, source_target_pairs={{0,8},{8,16},{16,24},{24,32},{32,40},{40,48},{48,56},{56,64},{64,7... | collective-permute-start | bytes 393224 | tf_op jit(solution)/shard_map/ppermute | solution.py:31
  153.0 18.4 %copy-start.70 = (f32[3,8,32,128]{3,2,1,0:T(8,128)}, f32[3,8,32,128]{3,2,1,0:T(8,128)S(1)}, u32[]{:S(2)}) copy-start(f32[3,8,32,128]{3,2,1,0:T(8,128)S(1)} %broadcast_multiply_fusion.3) | copy-start | bytes 1179652
  156.0 10.5 collective-permute-start.5
  172.6 140.3 %copy-start.81 = (s32[128]{0:T(128)S(1)}, s32[128]{0:T(128)}, u32[]{:S(2)}) copy-start(s32[128]{0:T(128)} %copy-done.80) | copy-start | bytes 1540
  239.5 71.6 %copy-start.59 = (f32[4,8,32,128]{3,2,1,0:T(8,128)}, f32[4,8,32,128]{3,2,1,0:T(8,128)S(1)}, u32[]{:S(2)}) copy-start(f32[4,8,32,128]{3,2,1,0:T(8,128)S(1)} %fusion.18) | copy-start | bytes 1572868
  307.3 7.3 copy-start.72
  315.6 4.4 copy-start.73
  321.9 15.0 collective-permute-start.6
  322.7 15.2 collective-permute-start.7
  327.5 5.6 collective-permute-start.8
  331.2 5.1 collective-permute-start.9
  406.4 3.6 copy-start.71
  407.0 75.3 %copy-start.82 = (s32[128]{0:T(128)S(1)}, s32[128]{0:T(128)}, u32[]{:S(2)}) copy-start(s32[128]{0:T(128)} %copy-done.80) | copy-start | bytes 1540
  482.3 3.5 copy-start.2
  490.7 16.1 collective-permute-start.10
  490.8 16.1 collective-permute-start.11
  496.6 8.8 collective-permute-start.12
  500.7 5.4 collective-permute-start.13
  579.1 75.0 %copy-start.83 = (s32[128]{0:T(128)S(1)}, s32[128]{0:T(128)}, u32[]{:S(2)}) copy-start(s32[128]{0:T(128)} %copy-done.80) | copy-start | bytes 1540
  662.5 15.7 collective-permute-start.14
  662.6 15.7 collective-permute-start.15
  668.4 8.4 collective-permute-start.16
  672.2 5.2 collective-permute-start.17
  751.7 74.2 %copy-start.84 = (s32[128]{0:T(128)S(1)}, s32[128]{0:T(128)}, u32[]{:S(2)}) copy-start(s32[128]{0:T(128)} %copy-done.80) | copy-start | bytes 1540
  825.9 4.1 copy-start.19
  835.8 15.8 collective-permute-start.18
  836.5 15.9 collective-permute-start.19
  842.2 7.7 collective-permute-start.20
  845.9 5.1 collective-permute-start.21
  926.8 74.8 %copy-start.85 = (s32[128]{0:T(128)S(1)}, s32[128]{0:T(128)}, u32[]{:S(2)}) copy-start(s32[128]{0:T(128)} %copy-done.80) | copy-start | bytes 1540
  1001.6 4.1 copy-start.27
  1010.9 16.1 collective-permute-start.22
  1011.7 16.1 collective-permute-start.23
  1017.4 7.6 collective-permute-start.24
  1021.2 5.1 collective-permute-start.25
  1179.1 4.2 copy-start.37
  1188.5 15.9 collective-permute-start.26
  1189.3 16.0 collective-permute-start.27
  1195.0 6.5 collective-permute-start.28
  1198.6 5.1 collective-permute-start.29
  1210.5 3.6 copy-start.35
  1282.6 74.8 %copy-start.86 = (s32[128]{0:T(128)S(1)}, s32[128]{0:T(128)}, u32[]{:S(2)}) copy-start(s32[128]{0:T(128)} %copy-done.80) | copy-start | bytes 1540
  1357.4 4.2 copy-start.45
  1366.7 14.9 collective-permute-start.30
  1367.0 14.8 collective-permute-start.31
  1372.7 7.2 collective-permute-start.32
  1376.5 5.1 collective-permute-start.33
  1386.1 4.2 copy-start.33
  1458.1 70.0 %copy-start.89 = (f32[256]{0:T(256)S(1)}, f32[256]{0:T(256)}, u32[]{:S(2)}) copy-start(f32[256]{0:T(256)} %pad.16.clone) | copy-start | bytes 3076
  1458.1 70.7 %copy-start.78 = (f32[32,32]{0,1:T(8,128)S(1)}, f32[32,32]{0,1:T(8,128)}, u32[]{:S(2)}) copy-start(f32[32,32]{0,1:T(8,128)} %get-tuple-element.346) | copy-start | bytes 12292
  1458.1 70.7 %copy-start.79 = (f32[32,32]{0,1:T(8,128)S(1)}, f32[32,32]{0,1:T(8,128)}, u32[]{:S(2)}) copy-start(f32[32,32]{0,1:T(8,128)} %slice_bitcast_fusion.30) | copy-start | bytes 12292
  1458.1 70.7 %copy-start.88 = (f32[256]{0:T(256)S(1)}, f32[256]{0:T(256)}, u32[]{:S(2)}) copy-start(f32[256]{0:T(256)} %pad.19.clone) | copy-start | bytes 3076
  1530.9 18.0 %copy-start.75 = (f32[32,32]{1,0:T(8,128)S(1)}, f32[32,32]{1,0:T(8,128)}, u32[]{:S(2)}) copy-start(f32[32,32]{1,0:T(8,128)} %copy-done.74) | copy-start | bytes 12292
  (61 other events, 119.6 us)
where the time goes:
time: 1630 us; the launch traced here: 1610 us
  blocking collectives  1090 us (67%)
  matrix products  178 us (11%)
  other arithmetic  138 us (8%)
  local copies, waits for them, and re-layouts  118 us (7%)
  starting transfers between devices  83.3 us (5%)
    psum x8, blocking collectives, per_device(): lax.psum(inner_local(image_block, image_block), ('lat', 'dep'))  511 us
    psum x8, blocking collectives, per_device(): coef_stack = lax.psum(local_prods, ('lat', 'dep'))  505 us
    psum x1, blocking collectives, per_device(): lax.psum(inner_local(rhs, rhs), ('lat', 'dep'))  68.8 us
    ppermute x16, starting transfers between devices, with_halo(): lax.ppermute(head, axis, [((i + 1) % count, i) for i in range(ends)])  54.5 us
    dot_general x52, matrix products, combine_columns(): return jnp.einsum('aevu,vw->aewu', vectors, matrix, precision=highest)  46.2 us
    another operation x7, other arithmetic, per_device(): jnp.linalg.cholesky(gram_small)  35.7 us
    dot_general x8, matrix products, apply_operator(): jnp.einsum('aeki,aevk->aevi', couple, near_traces, precision=highest)  34.6 us
    dot_general x8, matrix products, apply_operator(): jnp.einsum('aeij,aevj->aevi', diag_tiles, vectors, precision=highest)  33.2 us
  transfers between devices with their start and end apart: 34, of which 5 were waited for; matrix products, arithmetic and copies ran while one was open for 7% of the time, Pallas kernels for 0%

commit v1 on v0

--- a/solution.py
+++ b/solution.py
@@ -149,7 +149,9 @@
         coef_stack = lax.psum(local_prods, ("lat", "dep"))
         for prior in range(step_index + 1):
             image_block = image_block - combine_columns(basis_list[prior], coef_stack[prior])
-        gram_matrix = lax.psum(inner_local(image_block, image_block), ("lat", "dep"))
+        gram_matrix = jnp.sum(
+            lax.all_gather(inner_local(image_block, image_block), ("lat", "dep")), axis=0
+        )
         upper_factor, inverse = factor(gram_matrix)
         column_coefs = [coef_stack[prior] for prior in range(step_index + 1)]
         column_coefs.append(upper_factor)

time: 1630 us -> 1440 us (0.88)
  blocking collectives: 1090 us -> 885 us
    psum x8 -> x0, blocking collectives: 511 us -> none  [per_device(): lax.psum(inner_local(image_block, image_block), ('lat', 'dep'))]
    all_gather x0 -> x8, blocking collectives: none -> 310 us  [per_device(): lax.all_gather(inner_local(image_block, image_block), ('lat', 'dep'))]
  transfers between devices with their start and end apart: 34 -> 34, of which waited for: 5 -> 5; matrix products, arithmetic and copies ran while one was open for 7% -> 8% of each run, Pallas kernels for 0% -> 0%
where the time goes in v1:
time: 1440 us; the launch traced here: 1430 us
  blocking collectives  885 us (61%)
  matrix products  178 us (12%)
  other arithmetic  151 us (10%)
  local copies, waits for them, and re-layouts  118 us (8%)
  starting transfers between devices  85.4 us (6%)
    psum x8, blocking collectives, per_device(): coef_stack = lax.psum(local_prods, ('lat', 'dep'))  507 us
    all_gather x8, blocking collectives, per_device(): lax.all_gather(inner_local(image_block, image_block), ('lat', 'dep'))  310 us
    psum x1, blocking collectives, per_device(): lax.psum(inner_local(rhs, rhs), ('lat', 'dep'))  68.8 us
    ppermute x16, starting transfers between devices, with_halo(): lax.ppermute(head, axis, [((i + 1) % count, i) for i in range(ends)])  51.7 us
    dot_general x52, matrix products, combine_columns(): return jnp.einsum('aevu,vw->aewu', vectors, matrix, precision=highest)  46.2 us
    another operation x7, other arithmetic, per_device(): jnp.linalg.cholesky(gram_small)  35.9 us
    dot_general x8, matrix products, apply_operator(): jnp.einsum('aeki,aevk->aevi', couple, near_traces, precision=highest)  34.6 us
    dot_general x8, matrix products, apply_operator(): jnp.einsum('aeij,aevj->aevi', diag_tiles, vectors, precision=highest)  33.3 us
  transfers between devices with their start and end apart: 34, of which 5 were waited for; matrix products, arithmetic and copies ran while one was open for 8% of the time, Pallas kernels for 0%

profile of v1, /device:TPU:1, one launch (start us, length us, event | category | flops | bytes accessed | tf_op | source)
XLA Modules:
  0.0 1428.5 jit_solution(15465172937849154641)
XLA Ops:
  1.6 68.8 %psum.63 = f32[32,32]{0,1:T(8,128)S(1)} all-reduce(f32[32,32]{0,1:T(8,128)S(1)} %convolution_bitcast_fusion.97), channel_id=1, replica_groups=mesh['lat'=16,'dep'=8] {'lat','dep'}, use_global_device_ids=true, to_apply=%region_0.1 | all-reduce | flops 1024 | bytes 8192 | tf_op jit(solution)/shard_map/psum | solution.py:141
  70.5 2.9 cholesky.267
  79.9 4.8 collective-permute-start.1
  85.5 3.0 collective-permute-start.2
  91.3 50.8 %while.18 = (s32[]{:T(128)}, f32[4,8,128,128]{3,2,1,0:T(8,128)S(1)}, f32[4,8,128]{2,1,0:T(8,128)S(1)}, f32[3,64,64]{2,0,1:T(4,128)S(1)}, f32[4,8,128]{2,1,0:T(8,...) while((s32[]{:T(128)}, ...), condition=%wide.region_4.7_spmd.clone.clone, body=%wide.region_3.6_spmd.clone.clone.sunk | while | flops 63704832 | bytes 7220429 | solution.py:126
  93.0 3.4 convolution_bitcast_fusion.99
  105.7 3.4 convolution_bitcast_fusion.99
  118.4 3.4 convolution_bitcast_fusion.99
  131.1 3.4 convolution_bitcast_fusion.99
  149.2 4.1 fusion.395
  156.6 3.6 collective-permute-start.5
  167.7 4.3 convolution_subtract_fusion.7
  173.2 65.2 %psum.64 = f32[32,32]{0,1:T(8,128)S(1)} all-reduce(f32[32,32]{0,1:T(8,128)} %convolution_bitcast_fusion.95), channel_id=1, replica_groups=mesh['lat'=16,'dep'=8] {'lat','dep'}, use_global_device_ids=true, to_apply=%region_5.8 | all-reduce | flops 1024 | bytes 8192 | tf_op jit(solution)/shard_map/psum | solution.py:149
  240.6 38.7 %all-gather = f32[4096,32]{1,0:T(8,128)} all-gather(f32[32,32]{1,0:T(8,128)S(1)} %convolution_bitcast_fusion.94), channel_id=2, replica_groups=mesh['lat'=16,'dep'=8] {'lat','dep'}, dimensions={0}, use_global_device_ids=true | all-gather | bytes 528384 | tf_op jit(solution)/shard_map/all_gather | solution.py:153
  281.2 2.9 cholesky.278
  292.5 4.2 fusion.396
  299.9 4.2 collective-permute-start.7
  304.1 3.1 collective-permute-start.8
  314.9 4.3 convolution_subtract_fusion.6
  320.6 62.5 %psum.65 = f32[2,32,32]{1,2,0:T(8,128)S(1)} all-reduce(f32[2,32,32]{1,2,0:T(8,128)S(1)} %pad_maximum_fusion.5), channel_id=1, replica_groups=mesh['lat'=16,'dep'=8] {'lat','dep'}, use_global_device_ids=true, to_apply=%region_7.10 | all-reduce | flops 2048 | bytes 16384 | tf_op jit(solution)/shard_map/psum | solution.py:149
  386.7 38.6 %all-gather.1 = f32[4096,32]{1,0:T(8,128)} all-gather(f32[32,32]{1,0:T(8,128)S(1)} %convolution_bitcast_fusion.90), channel_id=3, replica_groups=mesh['lat'=16,'dep'=8] {'lat','dep'}, dimensions={0}, use_global_device_ids=true | all-gather | bytes 528384 | tf_op jit(solution)/shard_map/all_gather | solution.py:153
  427.3 2.9 cholesky.289
  439.2 4.2 fusion.397
  445.0 4.0 collective-permute-start.11
  450.0 3.3 collective-permute-start.12
  461.5 4.3 convolution_subtract_fusion.5
  467.7 63.4 %psum.66 = f32[3,32,32]{1,2,0:T(8,128)S(1)} all-reduce(f32[3,32,32]{1,2,0:T(8,128)S(1)} %pad_maximum_fusion.4), channel_id=1, replica_groups=mesh['lat'=16,'dep'=8] {'lat','dep'}, use_global_device_ids=true, to_apply=%region_9.12 | all-reduce | flops 3072 | bytes 24576 | tf_op jit(solution)/shard_map/psum | solution.py:149
  535.2 38.6 %all-gather.2 = f32[4096,32]{1,0:T(8,128)} all-gather(f32[32,32]{1,0:T(8,128)S(1)} %convolution_bitcast_fusion.85), channel_id=4, replica_groups=mesh['lat'=16,'dep'=8] {'lat','dep'}, dimensions={0}, use_global_device_ids=true | all-gather | bytes 528384 | tf_op jit(solution)/shard_map/all_gather | solution.py:153
  575.7 2.9 cholesky.300
  587.6 4.2 fusion.398
  592.7 4.7 collective-permute-start.15
  598.3 2.9 collective-permute-start.16
  609.3 4.3 convolution_subtract_fusion.4
  616.0 63.0 %psum.67 = f32[4,32,32]{1,2,0:T(8,128)S(1)} all-reduce(f32[4,32,32]{1,2,0:T(8,128)S(1)} %pad_maximum_fusion.3), channel_id=1, replica_groups=mesh['lat'=16,'dep'=8] {'lat','dep'}, use_global_device_ids=true, to_apply=%region_11.14 | all-reduce | flops 4096 | bytes 32768 | tf_op jit(solution)/shard_map/psum | solution.py:149
  683.9 38.6 %all-gather.3 = f32[4096,32]{1,0:T(8,128)} all-gather(f32[32,32]{1,0:T(8,128)S(1)} %convolution_bitcast_fusion.79), channel_id=5, replica_groups=mesh['lat'=16,'dep'=8] {'lat','dep'}, dimensions={0}, use_global_device_ids=true | all-gather | bytes 528384 | tf_op jit(solution)/shard_map/all_gather | solution.py:153
  736.9 4.2 fusion.399
  744.0 4.2 collective-permute-start.19
  749.1 3.2 collective-permute-start.20
  759.9 4.3 convolution_subtract_fusion.3
  767.2 63.2 %psum.68 = f32[5,32,32]{1,2,0:T(8,128)S(1)} all-reduce(f32[5,32,32]{1,2,0:T(8,128)S(1)} %fusion.76), channel_id=1, replica_groups=mesh['lat'=16,'dep'=8] {'lat','dep'}, use_global_device_ids=true, to_apply=%region_13.16 | all-reduce | flops 5120 | bytes 40960 | tf_op jit(solution)/shard_map/psum | solution.py:149
  835.9 38.7 %all-gather.4 = f32[4096,32]{1,0:T(8,128)} all-gather(f32[32,32]{1,0:T(8,128)S(1)} %convolution_bitcast_fusion.72), channel_id=6, replica_groups=mesh['lat'=16,'dep'=8] {'lat','dep'}, dimensions={0}, use_global_device_ids=true | all-gather | bytes 528384 | tf_op jit(solution)/shard_map/all_gather | solution.py:153
  889.1 4.2 fusion.400
  895.7 4.1 collective-permute-start.23
  900.7 3.1 collective-permute-start.24
  912.3 4.3 convolution_subtract_fusion.2
  920.2 63.2 %psum.69 = f32[6,32,32]{1,2,0:T(8,128)S(1)} all-reduce(f32[6,32,32]{1,2,0:T(8,128)S(1)} %fusion.70), channel_id=1, replica_groups=mesh['lat'=16,'dep'=8] {'lat','dep'}, use_global_device_ids=true, to_apply=%region_15.18 | all-reduce | flops 6144 | bytes 49152 | tf_op jit(solution)/shard_map/psum | solution.py:149
  989.5 38.9 %all-gather.5 = f32[4096,32]{1,0:T(8,128)} all-gather(f32[32,32]{1,0:T(8,128)S(1)} %convolution_bitcast_fusion.64), channel_id=7, replica_groups=mesh['lat'=16,'dep'=8] {'lat','dep'}, dimensions={0}, use_global_device_ids=true | all-gather | bytes 528384 | tf_op jit(solution)/shard_map/all_gather | solution.py:153
  1043.6 4.2 fusion.401
  1050.3 4.0 collective-permute-start.27
  1055.3 3.3 collective-permute-start.28
  1067.0 4.3 convolution_subtract_fusion.1
  1075.5 63.2 %psum.70 = f32[7,32,32]{1,2,0:T(8,128)S(1)} all-reduce(f32[7,32,32]{1,2,0:T(8,128)S(1)} %fusion.63), channel_id=1, replica_groups=mesh['lat'=16,'dep'=8] {'lat','dep'}, use_global_device_ids=true, to_apply=%region_17.20 | all-reduce | flops 7168 | bytes 57344 | tf_op jit(solution)/shard_map/psum | solution.py:149
  1145.4 38.7 %all-gather.6 = f32[4096,32]{1,0:T(8,128)} all-gather(f32[32,32]{1,0:T(8,128)S(1)} %convolution_bitcast_fusion.55), channel_id=8, replica_groups=mesh['lat'=16,'dep'=8] {'lat','dep'}, dimensions={0}, use_global_device_ids=true | all-gather | bytes 528384 | tf_op jit(solution)/shard_map/all_gather | solution.py:153
  1198.8 4.2 fusion.402
  1204.8 4.2 collective-permute-start.31
  1209.9 3.2 collective-permute-start.32
  1219.4 4.3 convolution_subtract_fusion
  1228.4 62.9 %psum.71 = f32[8,32,32]{1,2,0:T(8,128)S(1)} all-reduce(f32[8,32,32]{1,2,0:T(8,128)S(1)} %fusion.55), channel_id=1, replica_groups=mesh['lat'=16,'dep'=8] {'lat','dep'}, use_global_device_ids=true, to_apply=%region_19.22 | all-reduce | flops 8192 | bytes 65536 | tf_op jit(solution)/shard_map/psum | solution.py:149
  1296.8 38.6 %all-gather.7 = f32[4096,32]{1,0:T(8,128)} all-gather(f32[32,32]{1,0:T(8,128)S(1)} %convolution_bitcast_fusion.45), channel_id=9, replica_groups=mesh['lat'=16,'dep'=8] {'lat','dep'}, dimensions={0}, use_global_device_ids=true | all-gather | bytes 528384 | tf_op jit(solution)/shard_map/all_gather | solution.py:153
  1350.8 11.7 cholesky.77
  1365.4 9.8 custom-call.23
  1377.4 11.9 cholesky.132
  1394.2 5.1 while.17
  1399.3 20.5 %custom-call.24 = f32[2,128,128]{1,2,0:T(8,128)S(1)} custom-call(f32[2,128,128]{2,1,0:T(8,128)} %get-tuple-element.122), custom_call_target="InvertDiagBlocksLowerTriangular" | custom-call | tf_op jit(solution)/shard_map/jit(_cho_solve)/triangular_solve | solution.py:173
  (653 shorter events, 328.7 us)
Async XLA Ops:
  1.0 90.1 %copy-start.76 = (f32[3,64,64]{2,1,0:T(8,128)S(1)}, f32[3,64,64]{2,1,0:T(8,128)}, u32[]{:S(2)}) copy-start(f32[3,64,64]{2,1,0:T(8,128)} %param.14) | copy-start | bytes 147460
  1.6 89.7 %copy-start.87 = (f32[4,8,128]{2,1,0:T(8,128)S(1)}, f32[4,8,128]{2,1,0:T(8,128)}, u32[]{:S(2)}) copy-start(f32[4,8,128]{2,1,0:T(8,128)} %param.12) | copy-start | bytes 49156
  73.4 3.8 copy-start.74
  78.4 12.9 copy-start.51
  79.2 84.8 %collective-permute-start = (f32[1,8,1024]{2,1,0:T(8,128)}, f32[1,8,1024]{2,1,0:T(8,128)}, u32[]{:S(2)}, u32[]{:S(2)}) collective-permute-start(f32[1,8,1024]{2,1,0:T(8,128)} %slice.619), channel_id=1, source_target_pairs={{0,8},{8,16},{16,24},{24,32},{32,40},{40,48},{48,56},{56,64},{64,7... | collective-permute-start | bytes 98312 | tf_op jit(solution)/shard_map/ppermute | solution.py:19
  79.9 85.6 %collective-permute-start.1 = (f32[1,8,1024]{2,1,0:T(8,128)}, f32[1,8,1024]{2,1,0:T(8,128)}, u32[]{:S(2)}, u32[]{:S(2)}) collective-permute-start(f32[1,8,1024]{2,1,0:T(8,128)} %slice.623), channel_id=1, source_target_pairs={{8,0},{16,8},{24,16},{32,24},{40,32},{48,40},{56,48},{64,56},{72,6... | collective-permute-start | bytes 98312 | tf_op jit(solution)/shard_map/ppermute | solution.py:21
  85.5 71.1 %collective-permute-start.2 = (f32[1,4,1024]{2,1,0:T(4,128)}, f32[1,4,1024]{2,1,0:T(4,128)S(1)}, u32[]{:S(2)}, u32[]{:S(2)}) collective-permute-start(f32[1,4,1024]{2,1,0:T(4,128)} %slice.625), channel_id=1, source_target_pairs={{0,1},{1,2},{2,3},{3,4},{4,5},{5,6},{6,7},{8,9},{9,10},{10,11},{11... | collective-permute-start | bytes 49160 | tf_op jit(solution)/shard_map/ppermute | solution.py:19
  89.2 73.4 %collective-permute-start.3 = (f32[1,4,1024]{2,1,0:T(4,128)}, f32[1,4,1024]{2,1,0:T(4,128)}, u32[]{:S(2)}, u32[]{:S(2)}) collective-permute-start(f32[1,4,1024]{2,1,0:T(4,128)} %slice.629), channel_id=1, source_target_pairs={{1,0},{2,1},{3,2},{4,3},{5,4},{6,5},{7,6},{9,8},{10,9},{11,10},{12... | collective-permute-start | bytes 49160 | tf_op jit(solution)/shard_map/ppermute | solution.py:21
  91.3 50.8 %copy-start.77 = (f32[4,32,128]{2,1,0:T(8,128)S(1)}, f32[4,32,128]{2,1,0:T(8,128)}, u32[]{:S(2)}) copy-start(f32[4,32,128]{2,1,0:T(8,128)} %param.15) | copy-start | bytes 196612
  142.1 7.1 copy-start.80
  142.1 4.0 copy-start.52
  143.0 24.1 %collective-permute-start.4 = (f32[8,32,128]{2,1,0:T(8,128)}, f32[8,32,128]{2,1,0:T(8,128)}, u32[]{:S(2)}, u32[]{:S(2)}) collective-permute-start(f32[8,32,128]{2,1,0:T(8,128)} %broadcast_multiply_fusion.4), channel_id=1, source_target_pairs={{0,8},{8,16},{16,24},{24,32},{32,40},{40,48},{48,56},{56,64},{64,7... | collective-permute-start | bytes 393224 | tf_op jit(solution)/shard_map/ppermute | solution.py:31
  153.5 18.4 %copy-start.70 = (f32[3,8,32,128]{3,2,1,0:T(8,128)}, f32[3,8,32,128]{3,2,1,0:T(8,128)S(1)}, u32[]{:S(2)}) copy-start(f32[3,8,32,128]{3,2,1,0:T(8,128)S(1)} %broadcast_multiply_fusion.3) | copy-start | bytes 1179652
  156.6 10.5 collective-permute-start.5
  240.0 41.1 %copy-start.57 = (f32[4,8,32,128]{3,2,1,0:T(8,128)}, f32[4,8,32,128]{3,2,1,0:T(8,128)S(1)}, u32[]{:S(2)}) copy-start(f32[4,8,32,128]{3,2,1,0:T(8,128)S(1)} %fusion.18) | copy-start | bytes 1572868
  279.3 10.3 copy-start.81
  284.1 7.2 copy-start.72
  292.3 4.4 copy-start.73
  298.5 14.6 %collective-permute-start.6 = (f32[1,8,1024]{2,1,0:T(8,128)}, f32[1,8,1024]{2,1,0:T(8,128)}, u32[]{:S(2)}, u32[]{:S(2)}) collective-permute-start(f32[1,8,1024]{2,1,0:T(8,128)} %slice.641), channel_id=1, source_target_pairs={{0,8},{8,16},{16,24},{24,32},{32,40},{40,48},{48,56},{56,64},{64,7... | collective-permute-start | bytes 98312 | tf_op jit(solution)/shard_map/ppermute | solution.py:19
  299.9 14.1 collective-permute-start.7
  304.1 5.4 collective-permute-start.8
  307.4 5.1 collective-permute-start.9
  383.1 3.6 copy-start.71
  425.4 10.3 copy-start.82
  444.1 16.5 %collective-permute-start.10 = (f32[1,8,1024]{2,1,0:T(8,128)}, f32[1,8,1024]{2,1,0:T(8,128)S(1)}, u32[]{:S(2)}, u32[]{:S(2)}) collective-permute-start(f32[1,8,1024]{2,1,0:T(8,128)} %slice.655), channel_id=1, source_target_pairs={{0,8},{8,16},{16,24},{24,32},{32,40},{40,48},{48,56},{56,64},{64,7... | collective-permute-start | bytes 98312 | tf_op jit(solution)/shard_map/ppermute | solution.py:19
  445.0 15.6 %collective-permute-start.11 = (f32[1,8,1024]{2,1,0:T(8,128)S(1)}, f32[1,8,1024]{2,1,0:T(8,128)}, u32[]{:S(2)}, u32[]{:S(2)}) collective-permute-start(f32[1,8,1024]{2,1,0:T(8,128)S(1)} %slice.659), channel_id=1, source_target_pairs={{8,0},{16,8},{24,16},{32,24},{40,32},{48,40},{56,48},{64,56},{72,6... | collective-permute-start | bytes 98312 | tf_op jit(solution)/shard_map/ppermute | solution.py:21
  450.0 9.1 collective-permute-start.12
  454.2 5.6 collective-permute-start.13
  573.8 10.3 copy-start.83
  592.5 15.8 %collective-permute-start.14 = (f32[1,8,1024]{2,1,0:T(8,128)}, f32[1,8,1024]{2,1,0:T(8,128)S(1)}, u32[]{:S(2)}, u32[]{:S(2)}) collective-permute-start(f32[1,8,1024]{2,1,0:T(8,128)} %slice.670), channel_id=1, source_target_pairs={{0,8},{8,16},{16,24},{24,32},{32,40},{40,48},{48,56},{56,64},{64,7... | collective-permute-start | bytes 98312 | tf_op jit(solution)/shard_map/ppermute | solution.py:19
  592.7 15.7 %collective-permute-start.15 = (f32[1,8,1024]{2,1,0:T(8,128)S(1)}, f32[1,8,1024]{2,1,0:T(8,128)}, u32[]{:S(2)}, u32[]{:S(2)}) collective-permute-start(f32[1,8,1024]{2,1,0:T(8,128)S(1)} %slice.674), channel_id=1, source_target_pairs={{8,0},{16,8},{24,16},{32,24},{40,32},{48,40},{56,48},{64,56},{72,6... | collective-permute-start | bytes 98312 | tf_op jit(solution)/shard_map/ppermute | solution.py:21
  598.3 8.5 collective-permute-start.16
  602.2 5.4 collective-permute-start.17
  722.5 10.3 copy-start.84
  732.8 4.1 copy-start.19
  742.7 15.5 %collective-permute-start.18 = (f32[1,8,1024]{2,1,0:T(8,128)}, f32[1,8,1024]{2,1,0:T(8,128)}, u32[]{:S(2)}, u32[]{:S(2)}) collective-permute-start(f32[1,8,1024]{2,1,0:T(8,128)} %slice.686), channel_id=1, source_target_pairs={{0,8},{8,16},{16,24},{24,32},{32,40},{40,48},{48,56},{56,64},{64,7... | collective-permute-start | bytes 98312 | tf_op jit(solution)/shard_map/ppermute | solution.py:19
  744.0 15.1 %collective-permute-start.19 = (f32[1,8,1024]{2,1,0:T(8,128)}, f32[1,8,1024]{2,1,0:T(8,128)}, u32[]{:S(2)}, u32[]{:S(2)}) collective-permute-start(f32[1,8,1024]{2,1,0:T(8,128)} %slice.690), channel_id=1, source_target_pairs={{8,0},{16,8},{24,16},{32,24},{40,32},{48,40},{56,48},{64,56},{72,6... | collective-permute-start | bytes 98312 | tf_op jit(solution)/shard_map/ppermute | solution.py:21
  749.1 7.5 collective-permute-start.20
  752.4 5.1 collective-permute-start.21
  874.6 10.3 copy-start.85
  884.9 4.1 copy-start.27
  894.2 16.4 %collective-permute-start.22 = (f32[1,8,1024]{2,1,0:T(8,128)S(1)}, f32[1,8,1024]{2,1,0:T(8,128)}, u32[]{:S(2)}, u32[]{:S(2)}) collective-permute-start(f32[1,8,1024]{2,1,0:T(8,128)S(1)} %slice.703), channel_id=1, source_target_pairs={{0,8},{8,16},{16,24},{24,32},{32,40},{40,48},{48,56},{56,64},{64,7... | collective-permute-start | bytes 98312 | tf_op jit(solution)/shard_map/ppermute | solution.py:19
  895.7 15.8 %collective-permute-start.23 = (f32[1,8,1024]{2,1,0:T(8,128)}, f32[1,8,1024]{2,1,0:T(8,128)}, u32[]{:S(2)}, u32[]{:S(2)}) collective-permute-start(f32[1,8,1024]{2,1,0:T(8,128)} %slice.707), channel_id=1, source_target_pairs={{8,0},{16,8},{24,16},{32,24},{40,32},{48,40},{56,48},{64,56},{72,6... | collective-permute-start | bytes 98312 | tf_op jit(solution)/shard_map/ppermute | solution.py:21
  900.7 8.0 collective-permute-start.24
  904.8 5.1 collective-permute-start.25
  1039.4 4.2 copy-start.37
  1048.8 16.5 %collective-permute-start.26 = (f32[1,8,1024]{2,1,0:T(8,128)S(1)}, f32[1,8,1024]{2,1,0:T(8,128)}, u32[]{:S(2)}, u32[]{:S(2)}) collective-permute-start(f32[1,8,1024]{2,1,0:T(8,128)S(1)} %slice.721), channel_id=1, source_target_pairs={{0,8},{8,16},{16,24},{24,32},{32,40},{40,48},{48,56},{56,64},{64,7... | collective-permute-start | bytes 98312 | tf_op jit(solution)/shard_map/ppermute | solution.py:19
  1050.3 15.8 %collective-permute-start.27 = (f32[1,8,1024]{2,1,0:T(8,128)}, f32[1,8,1024]{2,1,0:T(8,128)}, u32[]{:S(2)}, u32[]{:S(2)}) collective-permute-start(f32[1,8,1024]{2,1,0:T(8,128)} %slice.725), channel_id=1, source_target_pairs={{8,0},{16,8},{24,16},{32,24},{40,32},{48,40},{56,48},{64,56},{72,6... | collective-permute-start | bytes 98312 | tf_op jit(solution)/shard_map/ppermute | solution.py:21
  1055.3 7.0 collective-permute-start.28
  1059.5 5.1 collective-permute-start.29
  1071.3 3.6 copy-start.35
  1139.3 3.5 copy-start.36
  1184.2 10.5 copy-start.86
  1194.6 4.1 copy-start.45
  1203.9 15.2 %collective-permute-start.30 = (f32[1,8,1024]{2,1,0:T(8,128)S(1)}, f32[1,8,1024]{2,1,0:T(8,128)S(1)}, u32[]{:S(2)}, u32[]{:S(2)}) collective-permute-start(f32[1,8,1024]{2,1,0:T(8,128)S(1)} %slice.740), channel_id=1, source_target_pairs={{0,8},{8,16},{16,24},{24,32},{32,40},{40,48},{48,56},{56,64},{64,7... | collective-permute-start | bytes 98312 | tf_op jit(solution)/shard_map/ppermute | solution.py:19
  1204.8 14.5 %collective-permute-start.31 = (f32[1,8,1024]{2,1,0:T(8,128)S(1)}, f32[1,8,1024]{2,1,0:T(8,128)S(1)}, u32[]{:S(2)}, u32[]{:S(2)}) collective-permute-start(f32[1,8,1024]{2,1,0:T(8,128)S(1)} %slice.744), channel_id=1, source_target_pairs={{8,0},{16,8},{24,16},{32,24},{40,32},{48,40},{56,48},{64,56},{72,6... | collective-permute-start | bytes 98312 | tf_op jit(solution)/shard_map/ppermute | solution.py:21
  1209.9 7.7 collective-permute-start.32
  1214.0 5.1 collective-permute-start.33
  1223.6 4.2 copy-start.33
  1296.8 45.4 %copy-start.89 = (f32[256]{0:T(256)S(1)}, f32[256]{0:T(256)}, u32[]{:S(2)}) copy-start(f32[256]{0:T(256)} %pad.16.clone) | copy-start | bytes 3076
  1296.8 46.2 %copy-start.78 = (f32[32,32]{0,1:T(8,128)S(1)}, f32[32,32]{0,1:T(8,128)}, u32[]{:S(2)}) copy-start(f32[32,32]{0,1:T(8,128)} %get-tuple-element.346) | copy-start | bytes 12292
  1296.8 46.2 %copy-start.79 = (f32[32,32]{0,1:T(8,128)S(1)}, f32[32,32]{0,1:T(8,128)}, u32[]{:S(2)}) copy-start(f32[32,32]{0,1:T(8,128)} %slice_bitcast_fusion.30) | copy-start | bytes 12292
  1296.8 46.2 %copy-start.88 = (f32[256]{0:T(256)S(1)}, f32[256]{0:T(256)}, u32[]{:S(2)}) copy-start(f32[256]{0:T(256)} %pad.19.clone) | copy-start | bytes 3076
  1345.0 18.0 %copy-start.75 = (f32[32,32]{1,0:T(8,128)S(1)}, f32[32,32]{1,0:T(8,128)}, u32[]{:S(2)}) copy-start(f32[32,32]{1,0:T(8,128)} %copy-done.74) | copy-start | bytes 12292
  (61 other events, 119.7 us)
